TPU v7x, 256 devices: a whole 4x4x8 slice. The times are simulated.
256 devices in a mesh: ctx: 64 (over z, y, core), head: 4 (over x).
Axes of the slice: x: 4, y: 4, z: 8, core: 2. Of those that a mesh axis runs over, the one named last changes fastest.
Arguments:
- queries: bfloat16 [32768, 32, 128], P(('ctx', 'head')), may hold values from -1.796875 to 1.796875
- key_vectors: bfloat16 [32768, 32, 128], P(('ctx', 'head')), may hold values from -1.796875 to 1.796875
- value_vectors: bfloat16 [32768, 32, 128], P(('ctx', 'head')), may hold values from -9.9 to 9.9
- output_grad: bfloat16 [32768, 32, 128], P(('ctx', 'head')), may hold values from -9.9 to 9.9
- decay_rate: float32 [32], replicated, may hold values from 0 to 1, as said below
- norm_gain: float32 [32, 128], replicated, may hold values from 0.25 to 1.75
Outputs:
- normed: bfloat16 [32768, 32, 128], P(('ctx', 'head'))
- query_gradient: bfloat16 [32768, 32, 128], P(('ctx', 'head'))
- grad_keys: bfloat16 [32768, 32, 128], P(('ctx', 'head'))
- value_gradient: bfloat16 [32768, 32, 128], P(('ctx', 'head'))
Inputs may be any that keep to these rules, and one draw needn't show every extreme that they name: `decay_rate`: each head's rate is positive; a head's state is multiplied by exp(-rate) at every position.
All inputs are finite; a program needn't handle non-finite values.
Results may differ from a plain program's by a relative error of at most 0.012.
Values may be sent and summed in bfloat16 or wider, within the bound.
A program may use at most 128 MiB of HBM per device.

v0:
```python
import jax
import jax.numpy as jnp
from jax import lax
from jax.sharding import PartitionSpec as P


def row_rates_here(head_rates, head_size, piece_rows):
    all_rates = jnp.repeat(head_rates, head_size)
    return lax.dynamic_slice_in_dim(all_rates, lax.axis_index("ctx") * piece_rows, piece_rows, 0)


def local_chain(spread_rows, rates_here, span_length, forward):
    row_decay = jnp.exp(-rates_here * span_length)[:, None]

    def carry_step(state, piece):
        return (row_decay * state + piece.astype(jnp.float32), state)

    empty_rows = jnp.zeros(spread_rows.shape[1:], jnp.float32)
    final_rows, carried_rows = lax.scan(carry_step, empty_rows, spread_rows, reverse=not forward)
    return carried_rows


def carry_states(stretch_states, head_rates, length, forward):
    group_size = stretch_states.shape[0]
    heads_here = stretch_states.shape[1]
    head_size = stretch_states.shape[2]
    stretch_order = jnp.arange(group_size).astype(jnp.float32)
    if forward:
        place_in = stretch_order
    else:
        place_in = group_size - 1.0 - stretch_order
    states_float = stretch_states.astype(jnp.float32)
    fold_weights = jnp.exp(-head_rates[None, :] * length * (group_size - 1.0 - place_in)[:, None])
    block_state = jnp.einsum("kh,khde->hde", fold_weights, states_float).astype(jnp.bfloat16)
    span_length = length * group_size
    total_rows = heads_here * head_size
    piece_rows = total_rows // lax.axis_size("ctx")
    flat_rows = block_state.reshape(1, total_rows, head_size)
    rates_here = row_rates_here(head_rates, head_size, piece_rows)
    if forward:
        spread_rows = lax.all_to_all(flat_rows, "ctx", split_axis=1, concat_axis=0, tiled=True)
        carried_rows = local_chain(spread_rows, rates_here, span_length, True)
        carried = (
            lax.all_to_all(
                carried_rows.astype(jnp.bfloat16), "ctx", split_axis=0, concat_axis=1, tiled=True
            )
            .astype(carried_rows.dtype)
            .reshape(heads_here, head_size, head_size)
        )
    else:
        spread_rows = lax.all_to_all(flat_rows, "ctx", split_axis=1, concat_axis=0, tiled=True)
        carried_rows = local_chain(spread_rows, rates_here, span_length, False)
        carried = (
            lax.all_to_all(
                carried_rows.astype(jnp.bfloat16), "ctx", split_axis=0, concat_axis=1, tiled=True
            )
            .astype(carried_rows.dtype)
            .reshape(heads_here, head_size, head_size)
        )
    lead_decay = jnp.exp(-head_rates[None, :] * length * place_in[:, None])
    stretch_gap = place_in[:, None] - 1.0 - place_in[None, :]
    inner_weights = jnp.where(
        (stretch_gap >= 0)[:, :, None],
        jnp.exp(-head_rates[None, None, :] * length * jnp.maximum(stretch_gap, 0.0)[:, :, None]),
        0.0,
    )
    spread = lead_decay[:, :, None, None] * carried[None] + jnp.einsum(
        "kqh,qhde->khde", inner_weights, states_float
    )
    return spread.astype(jnp.bfloat16)


def local(queries, key_vectors, value_vectors, output_grad, decay_rate, norm_gain):
    group_size = lax.axis_size("head")
    heads_group = decay_rate.shape[0] // group_size
    first_head = lax.axis_index("head") * heads_group
    group_rates = lax.dynamic_slice_in_dim(decay_rate, first_head, heads_group, 0)
    length = queries.shape[0]
    query_stretches = queries[None]
    key_stretches = key_vectors[None]
    value_stretches = value_vectors[None]
    grad_stretches = output_grad[None]
    steps = jnp.arange(length).astype(jnp.float32)
    offset = steps[:, None] - steps[None, :]
    decay_weight_mask = jnp.where(
        offset[None] >= 0, jnp.exp(-decay_rate[:, None, None] * jnp.maximum(offset, 0.0)[None]), 0.0
    )
    per_head_decay = jnp.exp(-decay_rate[None, :] * (steps[:, None] + 1.0))[None, :, :, None]
    trailing_decay = jnp.exp(-decay_rate[None, :] * (length - 1.0 - steps[:, None]))[
        None, :, :, None
    ]
    key_decayed = (key_stretches.astype(jnp.float32) * trailing_decay).astype(jnp.bfloat16)
    local_state = jnp.einsum(
        "kjhd,kjhe->khde", key_decayed, value_stretches, preferred_element_type=jnp.float32
    ).astype(jnp.bfloat16)
    owned_states = lax.all_to_all(local_state, "head", split_axis=1, concat_axis=0, tiled=True)
    incoming_portion = lax.all_to_all(
        carry_states(owned_states, group_rates, length, True),
        "head",
        split_axis=0,
        concat_axis=1,
        tiled=True,
    )
    scores = jnp.einsum(
        "kihd,kjhd->khij", query_stretches, key_stretches, preferred_element_type=jnp.float32
    )
    attention_matrix = (scores * decay_weight_mask[None]).astype(jnp.bfloat16)
    output_rows = jnp.einsum(
        "khij,kjhe->kihe", attention_matrix, value_stretches, preferred_element_type=jnp.float32
    )
    output_rows = output_rows + per_head_decay * jnp.einsum(
        "kihd,khde->kihe", query_stretches, incoming_portion, preferred_element_type=jnp.float32
    )
    inv_rms = lax.rsqrt(jnp.mean(output_rows * output_rows, axis=-1, keepdims=True) + 1e-06)
    unit_rows = output_rows * inv_rms
    gain_float = norm_gain[None, None]
    normed = (unit_rows * gain_float).astype(jnp.bfloat16)
    scaled = gain_float * grad_stretches.astype(jnp.float32)
    grad_out = (
        inv_rms * (scaled - unit_rows * jnp.mean(scaled * unit_rows, axis=-1, keepdims=True))
    ).astype(jnp.bfloat16)
    query_with_decay = (query_stretches.astype(jnp.float32) * per_head_decay).astype(jnp.bfloat16)
    state_gradient = jnp.einsum(
        "kihd,kihe->khde", query_with_decay, grad_out, preferred_element_type=jnp.float32
    ).astype(jnp.bfloat16)
    owned_grads = lax.all_to_all(state_gradient, "head", split_axis=1, concat_axis=0, tiled=True)
    later_portion = lax.all_to_all(
        carry_states(owned_grads, group_rates, length, False),
        "head",
        split_axis=0,
        concat_axis=1,
        tiled=True,
    )
    score_gradient = (
        jnp.einsum("kihe,kjhe->khij", grad_out, value_stretches, preferred_element_type=jnp.float32)
        * decay_weight_mask[None]
    ).astype(jnp.bfloat16)
    query_gradient = jnp.einsum(
        "khij,kjhd->kihd", score_gradient, key_stretches, preferred_element_type=jnp.float32
    )
    query_gradient = query_gradient + per_head_decay * jnp.einsum(
        "kihe,khde->kihd", grad_out, incoming_portion, preferred_element_type=jnp.float32
    )
    grad_keys = jnp.einsum(
        "khij,kihd->kjhd", score_gradient, query_stretches, preferred_element_type=jnp.float32
    )
    grad_keys = grad_keys + trailing_decay * jnp.einsum(
        "kjhe,khde->kjhd", value_stretches, later_portion, preferred_element_type=jnp.float32
    )
    value_gradient = jnp.einsum(
        "khij,kihe->kjhe", attention_matrix, grad_out, preferred_element_type=jnp.float32
    )
    value_gradient = value_gradient + trailing_decay * jnp.einsum(
        "kjhd,khde->kjhe", key_stretches, later_portion, preferred_element_type=jnp.float32
    )
    results = (
        normed,
        query_gradient.astype(jnp.bfloat16),
        grad_keys.astype(jnp.bfloat16),
        value_gradient.astype(jnp.bfloat16),
    )
    returned = (results[0][0], results[1][0], results[2][0], results[3][0])
    return returned


def solution(mesh):
    in_specs = (
        P(("ctx", "head"), None, None),
        P(("ctx", "head"), None, None),
        P(("ctx", "head"), None, None),
        P(("ctx", "head"), None, None),
        P(),
        P(),
    )
    out_specs = (
        P(("ctx", "head"), None, None),
        P(("ctx", "head"), None, None),
        P(("ctx", "head"), None, None),
        P(("ctx", "head"), None, None),
    )
    return jax.shard_map(local, mesh=mesh, in_specs=in_specs, out_specs=out_specs, check_vma=False)
```

profile of v0, /device:TPU:1, one launch (start us, length us, event | category | flops | bytes accessed | tf_op | source)
XLA Modules:
  0.0 292.3 jit_solution(5695599193048823478)
XLA Ops:
  5.2 4.8 %all-to-all-start = ((bf16[1,32,128,128]{3,2,0,1:T(8,128)(2,1)}), bf16[1,32,128,128]{3,2,0,1:T(8,128)(2,1)S(1)}, u32[]{:S(2)}, u32[]{:S(2)}) async-start(bf16[1,32,128,128]{3,2,0,1:T(8,128)(2,1)} %fusion.12), calls=%async_computation | async-start | bytes 2097152 | tf_op jit(solution)/shard_map/all_to_all | solution.py:96
  10.3 13.0 %all-to-all-done = bf16[1,32,128,128]{3,2,0,1:T(8,128)(2,1)S(1)} async-done(((bf16[1,32,128,128]{3,2,0,1:T(8,128)(2,1)}), bf16[1,32,128,128]{3,2,0,1:T(8,128)(2,1)S(1)}, u32[]{:S(2)}, u32[]{:S(2)}) %all-to-all-start) | async-done | bytes 1048608 | tf_op jit(solution)/shard_map/all_to_all | solution.py:96
  25.2 2.1 reduce.2
  28.1 14.5 %all-to-all-start.1 = ((bf16[64,2,1024]{2,1,0:T(2,128)(2,1)}), bf16[64,2,1024]{2,1,0:T(2,128)(2,1)S(1)}, u32[]{:S(2)}, u32[]{:S(2)}) async-start(bf16[64,2,1024]{2,1,0:T(2,128)(2,1)} %reshape.516), calls=%async_computation.1 | async-start | bytes 524288 | tf_op jit(solution)/shard_map/all_to_all | solution.py:41
  42.7 12.9 %all-to-all-done.1 = bf16[64,2,1024]{2,1,0:T(2,128)(2,1)S(1)} async-done(((bf16[64,2,1024]{2,1,0:T(2,128)(2,1)}), bf16[64,2,1024]{2,1,0:T(2,128)(2,1)S(1)}, u32[]{:S(2)}, u32[]{:S(2)}) %all-to-all-start.1) | async-done | bytes 262176 | tf_op jit(solution)/shard_map/all_to_all | solution.py:41
  56.7 43.0 %while.30 = (s32[]{:T(128)}, f32[16,128]{1,0:T(8,128)S(1)}, bf16[64,16,128]{2,1,0:T(8,128)(2,1)}, f32[16,1]{0,1:T(1,128)S(1)}, bf16[64,16,128]{2,1,0:T(8,128)(2,1)S(1)}, /*index=5*/s32[]{:T(128)}, s32[]{:T(128)}) while((s32[]{:T(128)}, f32[16,128]{1,0:T(8,128)S(1)}, bf16[64,16,128]{2,1,0:T(8,128)(2,1)}, f32[16,1]{0,1:T(1,128)S(1)}, ...), condition=%wide.region_1.2_spmd.clone, body=%wide.region_0.1_spmd.clone.sunk | while | flops 10243 | bytes 32936 | solution.py:19
  99.7 4.7 %all-to-all-start.2 = ((bf16[64,16,128]{2,1,0:T(8,128)(2,1)}), bf16[64,16,128]{2,1,0:T(8,128)(2,1)S(1)}, u32[]{:S(2)}, u32[]{:S(2)}) async-start(bf16[64,16,128]{2,1,0:T(8,128)(2,1)} %get-tuple-element.134), calls=%async_computation.2 | async-start | bytes 524288 | tf_op jit(solution)/shard_map/all_to_all | solution.py:44
  104.5 2.7 copy.119
  109.5 8.1 %all-to-all-done.2 = bf16[64,16,128]{2,1,0:T(8,128)(2,1)S(1)} async-done(((bf16[64,16,128]{2,1,0:T(8,128)(2,1)}), bf16[64,16,128]{2,1,0:T(8,128)(2,1)S(1)}, u32[]{:S(2)}, u32[]{:S(2)}) %all-to-all-start.2) | async-done | bytes 262176 | tf_op jit(solution)/shard_map/all_to_all | solution.py:44
  120.1 3.7 %all-to-all-start.3 = ((bf16[4,8,128,128]{3,2,1,0:T(8,128)(2,1)}), bf16[4,8,128,128]{3,2,1,0:T(8,128)(2,1)S(1)}, u32[]{:S(2)}, u32[]{:S(2)}) async-start(bf16[4,8,128,128]{3,2,1,0:T(8,128)(2,1)} %copy.116), calls=%async_computation.3 | async-start | bytes 2097152 | tf_op jit(solution)/shard_map/all_to_all | solution.py:97
  123.9 2.4 multiply_convert_fusion.4
  127.2 2.2 fusion.35
  129.5 9.0 %all-to-all-done.3 = bf16[4,8,128,128]{3,2,1,0:T(8,128)(2,1)S(1)} async-done(((bf16[4,8,128,128]{3,2,1,0:T(8,128)(2,1)}), bf16[4,8,128,128]{3,2,1,0:T(8,128)(2,1)S(1)}, u32[]{:S(2)}, u32[]{:S(2)}) %all-to-all-start.3) | async-done | bytes 1048608 | tf_op jit(solution)/shard_map/all_to_all | solution.py:97
  138.5 3.3 %multiply_reduce_fusion = (f32[128,32]{0,1:T(8,128)S(1)}, f32[1,128,32,128]{1,3,2,0:T(8,128)S(1)}) fusion(bf16[32,128,128]{2,1,0:T(8,128)(2,1)S(1)} %bitcast.189, bf16[128,32,128]{2,1,0:T(8,128)(2,1)} %param.10, f32[128,32]{0,1:T(8,128)S(1)} %get-tuple-element.215, f32[32,128,128]{1,2,0:T(8,128)} %fusion.35), kind=kOutput, calls=%fused_computation.28 | convolution fusion | flops 136310784 | bytes 6324224 | tf_op jit(solution)/shard_map/kihd,khde->kihe/dot_general | solution.py:111
  146.6 4.2 %all-to-all-start.4 = ((bf16[1,32,128,128]{3,2,0,1:T(8,128)(2,1)}), bf16[1,32,128,128]{3,2,0,1:T(8,128)(2,1)}, u32[]{:S(2)}, u32[]{:S(2)}) async-start(bf16[1,32,128,128]{3,2,0,1:T(8,128)(2,1)} %fusion.13), calls=%async_computation.4 | async-start | bytes 2097152 | tf_op jit(solution)/shard_map/all_to_all | solution.py:126
  150.8 14.1 %all-to-all-done.4 = bf16[1,32,128,128]{3,2,0,1:T(8,128)(2,1)} async-done(((bf16[1,32,128,128]{3,2,0,1:T(8,128)(2,1)}), bf16[1,32,128,128]{3,2,0,1:T(8,128)(2,1)}, u32[]{:S(2)}, u32[]{:S(2)}) %all-to-all-start.4) | async-done | bytes 1048608 | tf_op jit(solution)/shard_map/all_to_all | solution.py:126
  164.9 2.1 fusion.29
  168.3 3.0 %reduce.3 = bf16[1024,128]{1,0:T(8,128)(2,1)S(1)} reduce(bf16[1024,1,128]{2,1,0:T(2,128)(2,1)} %bitcast.194, bf16[]{:T(256)} %broadcast.338), dimensions={1}, to_apply=%bitcast.171.reduce_sub_computation | reduce | bytes 524290
  172.1 6.0 %all-to-all-start.5 = ((bf16[64,2,1024]{2,1,0:T(2,128)(2,1)}), bf16[64,2,1024]{2,1,0:T(2,128)(2,1)S(1)}, u32[]{:S(2)}, u32[]{:S(2)}) async-start(bf16[64,2,1024]{2,1,0:T(2,128)(2,1)} %reshape.518), calls=%async_computation.5 | async-start | bytes 524288 | tf_op jit(solution)/shard_map/all_to_all | solution.py:51
  178.9 12.5 %all-to-all-done.5 = bf16[64,2,1024]{2,1,0:T(2,128)(2,1)S(1)} async-done(((bf16[64,2,1024]{2,1,0:T(2,128)(2,1)}), bf16[64,2,1024]{2,1,0:T(2,128)(2,1)S(1)}, u32[]{:S(2)}, u32[]{:S(2)}) %all-to-all-start.5) | async-done | bytes 262176 | tf_op jit(solution)/shard_map/all_to_all | solution.py:51
  194.2 49.5 %while.31 = (s32[]{:T(128)}, f32[16,128]{1,0:T(8,128)S(1)}, bf16[64,16,128]{2,1,0:T(8,128)(2,1)S(1)}, f32[16,1]{0,1:T(1,128)S(1)}, bf16[64,16,128]{2,1,0:T(8,128)(2,1)}, /*index=5*/s32[]{:T(128)}, s32[]{:T(128)}, s32[]{:T(128)}) while((s32[]{:T(128)}, f32[16,128]{1,0:T(8,128)S(1)}, bf16[64,16,128]{2,1,0:T(8,128)(2,1)S(1)}, ...), condition=%wide.region_5.6_spmd.clone, body=%wide.region_4.5_spmd.clone.sunk | while | flops 10244 | bytes 32956 | solution.py:19
  244.4 4.7 %all-to-all-start.6 = ((bf16[64,16,128]{2,1,0:T(8,128)(2,1)}), bf16[64,16,128]{2,1,0:T(8,128)(2,1)S(1)}, u32[]{:S(2)}, u32[]{:S(2)}) async-start(bf16[64,16,128]{2,1,0:T(8,128)(2,1)} %copy-done.13), calls=%async_computation.6 | async-start | bytes 524288 | tf_op jit(solution)/shard_map/all_to_all | solution.py:54
  251.2 2.2 fusion.22
  253.4 8.9 %all-to-all-done.6 = bf16[64,16,128]{2,1,0:T(8,128)(2,1)S(1)} async-done(((bf16[64,16,128]{2,1,0:T(8,128)(2,1)}), bf16[64,16,128]{2,1,0:T(8,128)(2,1)S(1)}, u32[]{:S(2)}, u32[]{:S(2)}) %all-to-all-start.6) | async-done | bytes 262176 | tf_op jit(solution)/shard_map/all_to_all | solution.py:54
  262.3 2.4 fusion.7
  266.0 3.5 %all-to-all-start.7 = ((bf16[4,8,128,128]{3,2,1,0:T(8,128)(2,1)}), bf16[4,8,128,128]{3,2,1,0:T(8,128)(2,1)S(1)}, u32[]{:S(2)}, u32[]{:S(2)}) async-start(bf16[4,8,128,128]{3,2,1,0:T(8,128)(2,1)} %copy.133), calls=%async_computation.7 | async-start | bytes 2097152 | tf_op jit(solution)/shard_map/all_to_all | solution.py:127
  269.5 3.4 %fusion.14 = bf16[128,32,128]{0,2,1:T(8,128)(2,1)} fusion(bf16[32,128,128]{2,1,0:T(8,128)(2,1)} %bitcast.190, bf16[128,32,128]{0,2,1:T(8,128)(2,1)S(1)} %get-tuple-element.210, f32[32,128,128]{1,2,0:T(8,128)} %fusion.22, f32[128,32]{0,1:T(8,128)S(1)} %get-tuple-element.215), kind=kOutput, calls=%fused_computation.36 | convolution fusion | flops 135790592 | bytes 5259264 | tf_op jit(solution)/shard_map/kihe,khde->kihd/dot_general | solution.py:141
  272.8 2.6 copy.140
  275.5 2.6 copy.141
  278.1 3.7 %fusion.25 = f32[32,128,128]{2,1,0:T(8,128)} fusion(bf16[32,128,128]{2,1,0:T(8,128)(2,1)} %copy-done.10, bf16[128,32,128]{2,1,0:T(8,128)(2,1)} %param.10), kind=kOutput, calls=%fused_computation.47 | convolution fusion | flops 134217728 | bytes 4194304 | tf_op jit(solution)/shard_map/khij,kihd->kjhd/dot_general | solution.py:144
  281.8 2.2 fusion.58
  284.4 3.0 %fusion.15 = bf16[128,32,128]{2,0,1:T(8,128)(2,1)S(1)} fusion(bf16[32,128,128]{2,1,0:T(8,128)(2,1)S(1)} %bitcast.187, f32[32,128,128]{2,1,0:T(8,128)} %fusion.25, f32[128,32]{0,1:T(8,128)S(1)} %get-tuple-element.216, bf16[128,32,128]{2,1,0:T(8,128)(2,1)S(1)} %copy-done), kind=kOutput, calls=%fused_computation.37 | convolution fusion | flops 135790592 | bytes 5259264 | tf_op jit(solution)/shard_map/kjhe,khde->kjhd/dot_general | solution.py:147
  (346 shorter events, 126.2 us)
Async XLA Ops:
  0.6 2.7 copy-start
  3.3 6.7 %copy-start.16 = (f32[32]{0:T(128)S(1)}, f32[32]{0:T(128)}, u32[]{:S(2)}) copy-start(f32[32]{0:T(128)} %param.14) | copy-start | bytes 388
  5.2 18.1 %all-to-all-start = ((bf16[1,32,128,128]{3,2,0,1:T(8,128)(2,1)}), bf16[1,32,128,128]{3,2,0,1:T(8,128)(2,1)S(1)}, u32[]{:S(2)}, u32[]{:S(2)}) async-start(bf16[1,32,128,128]{3,2,0,1:T(8,128)(2,1)} %fusion.12), calls=%async_computation | async-start | bytes 2097152 | tf_op jit(solution)/shard_map/all_to_all | solution.py:96
  23.3 1.0 copy-start.11
  28.1 27.6 %all-to-all-start.1 = ((bf16[64,2,1024]{2,1,0:T(2,128)(2,1)}), bf16[64,2,1024]{2,1,0:T(2,128)(2,1)S(1)}, u32[]{:S(2)}, u32[]{:S(2)}) async-start(bf16[64,2,1024]{2,1,0:T(2,128)(2,1)} %reshape.516), calls=%async_computation.1 | async-start | bytes 524288 | tf_op jit(solution)/shard_map/all_to_all | solution.py:41
  55.9 52.1 %copy-start.5 = (bf16[128,32,128]{2,1,0:T(8,128)(2,1)S(1)}, bf16[128,32,128]{2,1,0:T(8,128)(2,1)}, u32[]{:S(2)}) copy-start(bf16[128,32,128]{2,1,0:T(8,128)(2,1)} %param.10) | copy-start | bytes 3145732
  99.7 17.9 %all-to-all-start.2 = ((bf16[64,16,128]{2,1,0:T(8,128)(2,1)}), bf16[64,16,128]{2,1,0:T(8,128)(2,1)S(1)}, u32[]{:S(2)}, u32[]{:S(2)}) async-start(bf16[64,16,128]{2,1,0:T(8,128)(2,1)} %get-tuple-element.134), calls=%async_computation.2 | async-start | bytes 524288 | tf_op jit(solution)/shard_map/all_to_all | solution.py:44
  104.4 13.2 %copy-start.12 = (bf16[1,32,128,128]{3,2,0,1:T(8,128)(2,1)S(1)}, bf16[1,32,128,128]{3,2,0,1:T(8,128)(2,1)}, u32[]{:S(2)}) copy-start(bf16[1,32,128,128]{3,2,0,1:T(8,128)(2,1)} %copy-done.11) | copy-start | bytes 3145732
  118.8 5.0 %copy-start.1 = (bf16[128,32,128]{2,1,0:T(8,128)(2,1)S(1)}, bf16[128,32,128]{2,1,0:T(8,128)(2,1)}, u32[]{:S(2)}) copy-start(bf16[128,32,128]{2,1,0:T(8,128)(2,1)} %param.11) | copy-start | bytes 3145732
  118.8 5.0 %copy-start.15 = (f32[128,128]{1,0:T(8,128)S(1)}, f32[128,128]{1,0:T(8,128)}, u32[]{:S(2)}) copy-start(f32[128,128]{1,0:T(8,128)} %subtract_maximum_fusion) | copy-start | bytes 196612
  120.1 18.5 %all-to-all-start.3 = ((bf16[4,8,128,128]{3,2,1,0:T(8,128)(2,1)}), bf16[4,8,128,128]{3,2,1,0:T(8,128)(2,1)S(1)}, u32[]{:S(2)}, u32[]{:S(2)}) async-start(bf16[4,8,128,128]{3,2,1,0:T(8,128)(2,1)} %copy.116), calls=%async_computation.3 | async-start | bytes 2097152 | tf_op jit(solution)/shard_map/all_to_all | solution.py:97
  126.2 1.0 copy-start.8
  138.5 3.3 %copy-start.3 = (bf16[4,8,128,128]{3,2,1,0:T(8,128)(2,1)}, bf16[4,8,128,128]{3,2,1,0:T(8,128)(2,1)S(1)}, u32[]{:S(2)}) copy-start(bf16[4,8,128,128]{3,2,1,0:T(8,128)(2,1)S(1)} %all-to-all-done.3) | copy-start | bytes 3145732
  138.5 3.4 %copy-start.4 = (bf16[128,32,128]{0,2,1:T(8,128)(2,1)S(1)}, bf16[128,32,128]{0,2,1:T(8,128)(2,1)}, u32[]{:S(2)}) copy-start(bf16[128,32,128]{0,2,1:T(8,128)(2,1)} %copy.119) | copy-start | bytes 3145732
  138.5 3.4 %copy-start.14 = (f32[32,128]{1,0:T(8,128)S(1)}, f32[32,128]{1,0:T(8,128)}, u32[]{:S(2)}) copy-start(f32[32,128]{1,0:T(8,128)} %param.15) | copy-start | bytes 49156
  142.7 2.1 copy-start.7
  146.6 18.4 %all-to-all-start.4 = ((bf16[1,32,128,128]{3,2,0,1:T(8,128)(2,1)}), bf16[1,32,128,128]{3,2,0,1:T(8,128)(2,1)}, u32[]{:S(2)}, u32[]{:S(2)}) async-start(bf16[1,32,128,128]{3,2,0,1:T(8,128)(2,1)} %fusion.13), calls=%async_computation.4 | async-start | bytes 2097152 | tf_op jit(solution)/shard_map/all_to_all | solution.py:126
  172.1 19.3 %all-to-all-start.5 = ((bf16[64,2,1024]{2,1,0:T(2,128)(2,1)}), bf16[64,2,1024]{2,1,0:T(2,128)(2,1)S(1)}, u32[]{:S(2)}, u32[]{:S(2)}) async-start(bf16[64,2,1024]{2,1,0:T(2,128)(2,1)} %reshape.518), calls=%async_computation.5 | async-start | bytes 524288 | tf_op jit(solution)/shard_map/all_to_all | solution.py:51
  243.7 0.7 copy-start.13
  244.4 17.9 %all-to-all-start.6 = ((bf16[64,16,128]{2,1,0:T(8,128)(2,1)}), bf16[64,16,128]{2,1,0:T(8,128)(2,1)S(1)}, u32[]{:S(2)}, u32[]{:S(2)}) async-start(bf16[64,16,128]{2,1,0:T(8,128)(2,1)} %copy-done.13), calls=%async_computation.6 | async-start | bytes 524288 | tf_op jit(solution)/shard_map/all_to_all | solution.py:54
  250.1 1.0 copy-start.10
  251.2 11.1 %copy-start.17 = (pred[4,4]{1,0:T(4,128)(4,1)S(1)}, pred[4,4]{1,0:T(4,128)(4,1)}, u32[]{:S(2)}) copy-start(pred[4,4]{1,0:T(4,128)(4,1)} %subtract_compare_fusion.1) | copy-start | bytes 52
  266.0 18.5 %all-to-all-start.7 = ((bf16[4,8,128,128]{3,2,1,0:T(8,128)(2,1)}), bf16[4,8,128,128]{3,2,1,0:T(8,128)(2,1)S(1)}, u32[]{:S(2)}, u32[]{:S(2)}) async-start(bf16[4,8,128,128]{3,2,1,0:T(8,128)(2,1)} %copy.133), calls=%async_computation.7 | async-start | bytes 2097152 | tf_op jit(solution)/shard_map/all_to_all | solution.py:127
  278.1 3.7 %copy-start.9 = (bf16[32,128,128]{2,1,0:T(8,128)(2,1)S(1)}, bf16[32,128,128]{2,1,0:T(8,128)(2,1)}, u32[]{:S(2)}) copy-start(bf16[32,128,128]{2,1,0:T(8,128)(2,1)} %copy-done.8) | copy-start | bytes 3145732
  284.4 4.6 %copy-start.6 = (f32[32,128,128]{1,2,0:T(8,128)S(1)}, f32[32,128,128]{1,2,0:T(8,128)}, u32[]{:S(2)}) copy-start(f32[32,128,128]{1,2,0:T(8,128)} %fusion.58) | copy-start | bytes 6291460
  287.4 1.7 copy-start.2
where the time goes:
time: 295 us; the launch traced here: 292 us
  other arithmetic  106 us (36%)
  waiting for transfers between devices  79 us (27%)
  starting transfers between devices  46.3 us (16%)
  matrix products  35.3 us (12%)
  local copies, waits for them, and re-layouts  24.2 us (8%)
    add x128, other arithmetic, carry_step(): return (row_decay * state + piece.astype(jnp.float32), state)  53.3 us
    dynamic_update_slice x128, other arithmetic, local_chain(): lax.scan(carry_step, empty_rows, spread_rows, reverse=not forward)  39 us
    all_to_all x2, waiting for transfers between devices, carry_states(): lax.all_to_all(flat_rows, 'ctx', split_axis=1, concat_axis=0, tiled=True)  25.4 us
    all_to_all x2, starting transfers between devices, carry_states(): lax.all_to_all(flat_rows, 'ctx', split_axis=1, concat_axis=0, tiled=True)  20.5 us
    unnamed x48, local copies, waits for them, and re-layouts  19.1 us
    all_to_all x2, waiting for transfers between devices, carry_states(): lax.all_to_all(carried_rows.astype(jnp.bfloat16), 'ctx', split_axis=0, co...  17 us
    all_to_all x1, waiting for transfers between devices, local(): lax.all_to_all(state_gradient, 'head', split_axis=1, concat_axis=0, tiled...  14.1 us
    all_to_all x1, waiting for transfers between devices, local(): lax.all_to_all(local_state, 'head', split_axis=1, concat_axis=0, tiled=True)  13 us
  transfers between devices with their start and end apart: 8, of which 8 were waited for; matrix products, arithmetic and copies ran while one was open for 10% of the time, Pallas kernels for 0%

commit v1 on v0

v1 whole, which is shorter than its diff:
```python
import functools

import jax
import jax.numpy as jnp
from jax import lax
from jax.experimental import pallas as pl
from jax.experimental.pallas import tpu as pltpu
from jax.sharding import PartitionSpec as P

MESH = pl.DeviceIdType.MESH
NZ, NY, NCORE, NX = 8, 4, 2, 4
ROW = NCORE * NX
PER = 4
F32 = jnp.float32
BF16 = jnp.bfloat16


def dot(a, b, ca, cb):
    return lax.dot_general(a, b, (((ca,), (cb,)), ((), ())), preferred_element_type=F32)


def near_first(i):
    a = i // 2
    return (a * (a + 1) // 2) % 4 + 4 * (i % 2)


def kernel(
    rate_ref, gain_ref, q_ref, k_ref, v_ref, g_ref,
    normed_ref, dq_ref, dk_ref, dv_ref,
    att, intra, go, dk_part, dv_part, total,
    ls, lr, ts, tr, cs, cr, rs_, rr, ins, inr,
    gs, gr, tsb, trb, csb, crb, rsb, rrb, lts, ltr,
    s_l, r_l, s_t, r_t, s_c, r_c, s_r, r_r, s_i, r_i,
    s_lb, r_lb, s_tb, r_tb, s_cb, r_cb, s_rb, r_rb, s_ib, r_ib,
):
    ctx = lax.axis_index("ctx")
    x = lax.axis_index("head")
    z, y, core = ctx // (NY * NCORE), (ctx // NCORE) % NY, ctx % NCORE
    r = core * NX + x
    size = q_ref.shape[1]

    def row_device(r2):
        return ((z * NY + y) * NCORE + r2 // NX, r2 % NX)

    def y_device(y2):
        return ((z * NY + y2) * NCORE + core, x)

    def z_device(z2):
        return ((z2 * NY + y) * NCORE + core, x)

    barrier = pltpu.get_barrier_semaphore()

    @pl.loop(1, ROW)
    def _(o):
        pl.semaphore_signal(barrier, inc=1, device_id=row_device((r + o) % ROW), device_id_type=MESH)

    @pl.loop(1, NY)
    def _(o):
        pl.semaphore_signal(barrier, inc=1, device_id=y_device((y + o) % NY), device_id_type=MESH)

    @pl.loop(1, NZ)
    def _(o):
        pl.semaphore_signal(barrier, inc=1, device_id=z_device((z + o) % NZ), device_id_type=MESH)

    pl.semaphore_wait(barrier, ROW + NY + NZ - 3)

    step_i = lax.broadcasted_iota(jnp.int32, (size, size), 0).astype(F32)
    step_j = lax.broadcasted_iota(jnp.int32, (size, size), 1).astype(F32)
    offset = step_i - step_j

    def mask(rate):
        return jnp.where(offset >= 0, jnp.exp(-rate * jnp.maximum(offset, 0.0)), 0.0)

    def head_decay(rate):
        return jnp.exp(-rate * (step_i + 1.0))

    def tail_decay(rate):
        return jnp.exp(-rate * (size - 1.0 - step_i))

    def span_decay(rate, stretches):
        return jnp.exp(jnp.full((1, size), -rate * (1.0 * size * stretches), F32))

    def row_copy(src, dst, s_sem, r_sem, o):
        r2 = (r + o) % ROW
        return pltpu.make_async_remote_copy(
            src_ref=src.at[r2], dst_ref=dst.at[r], send_sem=s_sem.at[o], recv_sem=r_sem.at[o],
            device_id=row_device(r2), device_id_type=MESH)

    def row_send(src, dst, s_sem, r_sem, o):
        @pl.when(o != 0)
        def _():
            row_copy(src, dst, s_sem, r_sem, o).start()

        @pl.when(o == 0)
        def _():
            pltpu.make_async_copy(src.at[r], dst.at[r], r_sem.at[0]).start()

    def row_arrived(src, dst, s_sem, r_sem, o):
        r2 = (r + ROW - o) % ROW

        @pl.when(o != 0)
        def _():
            pltpu.make_async_remote_copy(
                src_ref=src.at[r2], dst_ref=dst.at[r2], send_sem=s_sem.at[o], recv_sem=r_sem.at[o],
                device_id=row_device(r2), device_id_type=MESH).wait_recv()

        @pl.when(o == 0)
        def _():
            pltpu.make_async_copy(src.at[r], dst.at[r], r_sem.at[0]).wait()

    def y_copy(src, dst, s_sem, r_sem, o, sending):
        y2 = (y + o) % NY if sending else (y + NY - o) % NY
        return pltpu.make_async_remote_copy(
            src_ref=src.at[y2], dst_ref=dst.at[y if sending else y2],
            send_sem=s_sem.at[o], recv_sem=r_sem.at[o],
            device_id=y_device(y2), device_id_type=MESH)

    def z_copy(src, dst, s_sem, r_sem, o, to_later):
        z2 = z + o if to_later else z - o
        return pltpu.make_async_remote_copy(
            src_ref=src, dst_ref=dst.at[z], send_sem=s_sem.at[o], recv_sem=r_sem.at[o],
            device_id=z_device(z2), device_id_type=MESH)

    def z_arrival(src, dst, s_sem, r_sem, o, to_later):
        z2 = z - o if to_later else z + o
        return pltpu.make_async_remote_copy(
            src_ref=src, dst_ref=dst.at[z2], send_sem=s_sem.at[o], recv_sem=r_sem.at[o],
            device_id=z_device(z2), device_id_type=MESH)

    def z_inside(o, later):
        return z + o < NZ if later else z - o >= 0

    def carry(own, got, t_out, t_in, c_out, c_in, r_out, r_in, out, back,
              s_own, r_own, s_t2, r_t2, s_c2, r_c2, s_r2, r_r2, s_out, r_out2, forward):
        @pl.loop(0, ROW)
        def _(i):
            row_arrived(own, got, s_own, r_own, near_first(i))

        order = range(ROW) if forward else range(ROW - 1, -1, -1)

        @pl.loop(0, PER)
        def _(j):
            weight = span_decay(rate_ref[r * PER + j], 1)
            acc = None
            for c in order:
                piece = got[c, j].astype(F32)
                acc = piece if acc is None else acc * weight + piece
            t_out[j] = acc.astype(BF16)

        @pl.loop(1, NY)
        def _(o):
            y_copy(t_out, t_in, s_t2, r_t2, o, True).start()

        t_in[y] = t_out[y]

        @pl.loop(1, NY)
        def _(o):
            y_copy(t_out, t_in, s_t2, r_t2, o, False).wait_recv()

        rate = rate_ref[r * PER + y]
        weight = span_decay(rate, ROW)
        acc = None
        y_order = range(NY) if forward else range(NY - 1, -1, -1)
        for c in y_order:
            piece = t_in[c].astype(F32)
            acc = piece if acc is None else acc * weight + piece
        c_out[...] = acc.astype(BF16)

        @pl.loop(1, NZ)
        def _(o):
            @pl.when(z_inside(o, forward))
            def _():
                z_copy(c_out, c_in, s_c2, r_c2, o, forward).start()

        total[...] = jnp.zeros_like(total)
        column = span_decay(rate, ROW * NY)

        @pl.loop(0, NZ - 1)
        def _(i):
            o = NZ - 1 - i

            @pl.when(z_inside(o, not forward))
            def _():
                z_arrival(c_out, c_in, s_c2, r_c2, o, forward).wait_recv()
                z2 = z - o if forward else z + o
                total[...] = total[...] * column + c_in[z2].astype(F32)

        acc = total[...]
        for c in y_order:
            r_out[c] = acc.astype(BF16)
            acc = acc * weight + t_in[c].astype(F32)

        @pl.loop(1, NY)
        def _(o):
            y_copy(r_out, r_in, s_r2, r_r2, o, True).start()

        r_in[y] = r_out[y]

        @pl.loop(1, NY)
        def _(o):
            y_copy(r_out, r_in, s_r2, r_r2, o, False).wait_recv()

        @pl.loop(0, PER)
        def _(j):
            weight = span_decay(rate_ref[r * PER + j], 1)
            acc = r_in[j].astype(F32)
            for c in order:
                out[c, j] = acc.astype(BF16)
                acc = acc * weight + got[c, j].astype(F32)

        @pl.loop(0, ROW)
        def _(i):
            row_send(out, back, s_out, r_out2, near_first(ROW - 1 - i))

    @pl.loop(0, ROW)
    def _(i):
        o = near_first(ROW - 1 - i)
        r2 = (r + o) % ROW
        for j in range(PER):
            h = r2 * PER + j
            rate = rate_ref[h]
            key_decayed = (k_ref[h].astype(F32) * tail_decay(rate)).astype(BF16)
            ls[r2, j] = dot(key_decayed, v_ref[h], 0, 0).astype(BF16)
        row_send(ls, lr, s_l, r_l, o)

    @pl.loop(0, ROW)
    def _(i):
        for j in range(PER):
            h = i * PER + j
            scores = dot(q_ref[h], k_ref[h], 1, 1)
            weights = (scores * mask(rate_ref[h])).astype(BF16)
            att[h] = weights
            intra[h] = dot(weights, v_ref[h], 1, 0)

    carry(ls, lr, ts, tr, cs, cr, rs_, rr, ins, inr,
          s_l, r_l, s_t, r_t, s_c, r_c, s_r, r_r, s_i, r_i, True)

    @pl.loop(0, ROW)
    def _(i):
        o = near_first(i)
        row_arrived(ins, inr, s_i, r_i, o)
        r2 = (r + ROW - o) % ROW
        for j in range(PER):
            h = r2 * PER + j
            decay = head_decay(rate_ref[h])
            queries = q_ref[h]
            outputs = intra[h] + decay * dot(queries, inr[r2, j], 1, 0)
            inv_rms = lax.rsqrt(jnp.mean(outputs * outputs, axis=-1, keepdims=True) + 1e-06)
            unit = outputs * inv_rms
            gain = gain_ref[h]
            normed_ref[h] = (unit * gain).astype(BF16)
            scaled = gain * g_ref[h].astype(F32)
            grad_out = (
                inv_rms * (scaled - unit * jnp.mean(scaled * unit, axis=-1, keepdims=True))
            ).astype(BF16)
            go[h] = grad_out
            query_decayed = (queries.astype(F32) * decay).astype(BF16)
            gs[r2, j] = dot(query_decayed, grad_out, 0, 0).astype(BF16)
        row_send(gs, gr, s_lb, r_lb, (ROW - o) % ROW)

    @pl.loop(0, ROW)
    def _(i):
        for j in range(PER):
            h = i * PER + j
            rate = rate_ref[h]
            grad_out = go[h]
            queries = q_ref[h]
            score_grad = (dot(grad_out, v_ref[h], 1, 1) * mask(rate)).astype(BF16)
            dq = dot(score_grad, k_ref[h], 1, 0)
            dq = dq + head_decay(rate) * dot(grad_out, inr[i, j], 1, 1)
            dq_ref[h] = dq.astype(BF16)
            dk_part[h] = dot(score_grad, queries, 0, 0)
            dv_part[h] = dot(att[h], grad_out, 0, 0)

    carry(gs, gr, tsb, trb, csb, crb, rsb, rrb, lts, ltr,
          s_lb, r_lb, s_tb, r_tb, s_cb, r_cb, s_rb, r_rb, s_ib, r_ib, False)

    @pl.loop(0, ROW)
    def _(i):
        o = near_first(i)
        row_arrived(lts, ltr, s_ib, r_ib, o)
        r2 = (r + ROW - o) % ROW
        for j in range(PER):
            h = r2 * PER + j
            decay = tail_decay(rate_ref[h])
            later = ltr[r2, j]
            dk_ref[h] = (dk_part[h] + decay * dot(v_ref[h], later, 1, 1)).astype(BF16)
            dv_ref[h] = (dv_part[h] + decay * dot(k_ref[h], later, 1, 0)).astype(BF16)

    @pl.loop(1, ROW)
    def _(o):
        row_copy(ls, lr, s_l, r_l, o).wait_send()
        row_copy(ins, inr, s_i, r_i, o).wait_send()
        row_copy(gs, gr, s_lb, r_lb, o).wait_send()
        row_copy(lts, ltr, s_ib, r_ib, o).wait_send()

    @pl.loop(1, NY)
    def _(o):
        y_copy(ts, tr, s_t, r_t, o, True).wait_send()
        y_copy(rs_, rr, s_r, r_r, o, True).wait_send()
        y_copy(tsb, trb, s_tb, r_tb, o, True).wait_send()
        y_copy(rsb, rrb, s_rb, r_rb, o, True).wait_send()

    @pl.loop(1, NZ)
    def _(o):
        @pl.when(z_inside(o, True))
        def _():
            z_copy(cs, cr, s_c, r_c, o, True).wait_send()

        @pl.when(z_inside(o, False))
        def _():
            z_copy(csb, crb, s_cb, r_cb, o, False).wait_send()


def local(queries, key_vectors, value_vectors, output_grad, decay_rate, norm_gain):
    length, heads, size = queries.shape
    by_head = [jnp.transpose(a, (1, 0, 2)) for a in (queries, key_vectors, value_vectors, output_grad)]
    tile = (size, size)
    whole = pl.BlockSpec(memory_space=pltpu.VMEM)
    one_way = [
        pltpu.VMEM((ROW, PER) + tile, BF16),
        pltpu.VMEM((ROW, PER) + tile, BF16),
        pltpu.VMEM((NY,) + tile, BF16),
        pltpu.VMEM((NY,) + tile, BF16),
        pltpu.VMEM(tile, BF16),
        pltpu.VMEM((NZ,) + tile, BF16),
        pltpu.VMEM((NY,) + tile, BF16),
        pltpu.VMEM((NY,) + tile, BF16),
        pltpu.VMEM((ROW, PER) + tile, BF16),
        pltpu.VMEM((ROW, PER) + tile, BF16),
    ]
    sems = [pltpu.SemaphoreType.DMA((n,)) for n in (ROW, ROW, NY, NY, NZ, NZ, NY, NY, ROW, ROW)]
    results = pl.pallas_call(
        kernel,
        out_shape=[jax.ShapeDtypeStruct((heads, length, size), BF16)] * 4,
        in_specs=[pl.BlockSpec(memory_space=pltpu.SMEM)] + [whole] * 5,
        out_specs=[whole] * 4,
        scratch_shapes=[
            pltpu.VMEM((heads,) + tile, BF16),
            pltpu.VMEM((heads,) + tile, F32),
            pltpu.VMEM((heads,) + tile, BF16),
            pltpu.VMEM((heads,) + tile, F32),
            pltpu.VMEM((heads,) + tile, F32),
            pltpu.VMEM(tile, F32),
        ] + one_way + one_way + sems + sems,
        compiler_params=pltpu.CompilerParams(
            collective_id=0, has_side_effects=True, vmem_limit_bytes=60 * 1024 * 1024
        ),
    )(decay_rate, norm_gain.reshape(heads, 1, size), *by_head)
    return tuple(jnp.transpose(a, (1, 0, 2)) for a in results)


def solution(mesh):
    spec = P(("ctx", "head"), None, None)
    return jax.shard_map(
        local, mesh=mesh, in_specs=(spec,) * 4 + (P(), P()), out_specs=(spec,) * 4, check_vma=False
    )
```

time: 295 us -> 114 us (0.39)
  other arithmetic: 106 us -> 0 us
  Pallas kernels: 0 us -> 98.7 us
  waiting for transfers between devices: 79 us -> 0 us
  starting transfers between devices: 46.3 us -> 0 us
  matrix products: 35.3 us -> 0 us
  local copies, waits for them, and re-layouts: 24.2 us -> 13.9 us
    pallas_call x0 -> x1, Pallas kernels: none -> 98.7 us  [local(): pl.pallas_call(kernel, out_shape=[jax.ShapeDtypeStruct((heads, length, si...]
    all_to_all x8 -> x0, waiting for transfers between devices: 79 us -> none  [the longest x2 25.4 us: carry_states(): lax.all_to_all(flat_rows, 'ctx', split_axis=1, concat_axis=0, tiled=True)]
    add x128 -> x0, other arithmetic: 53.3 us -> none  [carry_step(): return (row_decay * state + piece.astype(jnp.float32), state)]
    all_to_all x8 -> x0, starting transfers between devices: 46.3 us -> none  [the longest x2 20.5 us: carry_states(): lax.all_to_all(flat_rows, 'ctx', split_axis=1, concat_axis=0, tiled=True)]
    dynamic_update_slice x128 -> x0, other arithmetic: 39 us -> none  [local_chain(): lax.scan(carry_step, empty_rows, spread_rows, reverse=not forward)]
    dot_general x16 -> x0, matrix products: 35.3 us -> none  [the longest x1 3.69 us: local(): jnp.einsum('khij,kihd->kjhd', score_gradient, query_stretches, preferred_...]
    unnamed x48 -> x14, local copies, waits for them, and re-layouts: 19.1 us -> 7.93 us
    transpose x0 -> x2, local copies, waits for them, and re-layouts: none -> 5.94 us  [local(): jnp.transpose(a, (1, 0, 2))]
  transfers between devices with their start and end apart: 8 -> 0, of which waited for: 8 -> 0; matrix products, arithmetic and copies ran while one was open for 10% -> 0% of each run, Pallas kernels for 0% -> 0%
where the time goes in v1:
time: 114 us; the launch traced here: 113 us
  Pallas kernels  98.7 us (87%)
  local copies, waits for them, and re-layouts  13.9 us (12%)
    pallas_call x1, Pallas kernels, local(): pl.pallas_call(kernel, out_shape=[jax.ShapeDtypeStruct((heads, length, si...  98.7 us
    unnamed x14, local copies, waits for them, and re-layouts  7.93 us
    transpose x2, local copies, waits for them, and re-layouts, local(): jnp.transpose(a, (1, 0, 2))  5.94 us

profile of v1, /device:TPU:1, one launch (start us, length us, event | category | flops | bytes accessed | tf_op | source)
XLA Modules:
  0.0 113.2 jit_solution(13151184027746418152)
XLA Ops:
  0.6 0.0 copy-start.3
  0.6 0.0 copy-start.4
  0.7 3.8 %copy_bitcast_fusion.2 = (bf16[32,128,128]{2,1,0:T(8,128)(2,1)}, bf16[32,128,128]{2,1,0:T(8,128)(2,1)}) fusion(bf16[128,32,128]{2,1,0:T(8,128)(2,1)} %param.7, bf16[128,32,128]{2,1,0:T(8,128)(2,1)} %param.6), kind=kLoop, calls=%fused_computation.2 | loop fusion | bytes 4194304 | tf_op jit(solution)/shard_map/transpose | solution.py:317
  4.5 0.0 copy-done.3
  4.5 0.0 copy-done.4
  4.5 2.1 %copy_bitcast_fusion = (bf16[32,128,128]{2,1,0:T(8,128)(2,1)}, bf16[32,128,128]{2,1,0:T(8,128)(2,1)}) fusion(bf16[128,32,128]{2,1,0:T(8,128)(2,1)S(1)} %copy-done.3, bf16[128,32,128]{2,1,0:T(8,128)(2,1)S(1)} %copy-done.4), kind=kLoop, calls=%fused_computation | loop fusion | bytes 4194304 | tf_op jit(solution)/shard_map/transpose | solution.py:317
  6.6 98.7 %shard_map.93 = (bf16[32,128,128]{2,1,0:T(8,128)(2,1)}, bf16[32,128,128]{2,1,0:T(8,128)(2,1)}, bf16[32,128,128]{2,1,0:T(8,128)(2,1)}, bf16[32,128,128]{2,1,0:T(8,128)(2,1)}) custom-call(f32[32]{0:T(128)} %rate_ref.1, f32[32,1,128]{2,1,0:T(1,128)} %bitcast.17, bf16[32,128,128]{2,1,0:T(8,128)(2,1)} %get-tuple-element.19.q_ref, ...), custom_call_target="tpu_custom_call" | custom-call | tf_op jit(solution)/shard_map/pallas_call | solution.py:333
  105.3 0.0 copy-start.2
  105.3 3.0 %copy.14 = bf16[128,32,128]{2,1,0:T(8,128)(2,1)} copy(bf16[128,32,128]{2,0,1:T(8,128)(2,1)} %bitcast.16) | data formatting | bytes 2097152
  108.2 0.0 copy-done.2
  108.2 0.0 copy-start.1
  108.2 1.6 %copy.15 = bf16[128,32,128]{2,1,0:T(8,128)(2,1)} copy(bf16[128,32,128]{2,0,1:T(8,128)(2,1)S(1)} %bitcast.15) | data formatting | bytes 2097152
  109.9 0.0 copy-done.1
  109.9 0.0 copy-start
  109.9 1.6 %copy.16 = bf16[128,32,128]{2,1,0:T(8,128)(2,1)} copy(bf16[128,32,128]{2,0,1:T(8,128)(2,1)S(1)} %bitcast.14) | data formatting | bytes 2097152
  111.6 0.0 copy-done
  111.6 1.6 %copy.17 = bf16[128,32,128]{2,1,0:T(8,128)(2,1)} copy(bf16[128,32,128]{2,0,1:T(8,128)(2,1)S(1)} %bitcast.13) | data formatting | bytes 2097152
Async XLA Ops:
  0.6 3.8 %copy-start.3 = (bf16[128,32,128]{2,1,0:T(8,128)(2,1)S(1)}, bf16[128,32,128]{2,1,0:T(8,128)(2,1)}, u32[]{:S(2)}) copy-start(bf16[128,32,128]{2,1,0:T(8,128)(2,1)} %param.9) | copy-start | bytes 3145732
  0.6 3.8 %copy-start.4 = (bf16[128,32,128]{2,1,0:T(8,128)(2,1)S(1)}, bf16[128,32,128]{2,1,0:T(8,128)(2,1)}, u32[]{:S(2)}) copy-start(bf16[128,32,128]{2,1,0:T(8,128)(2,1)} %param.8) | copy-start | bytes 3145732
  105.3 3.0 %copy-start.2 = (bf16[32,128,128]{2,1,0:T(8,128)(2,1)S(1)}, bf16[32,128,128]{2,1,0:T(8,128)(2,1)}, u32[]{:S(2)}) copy-start(bf16[32,128,128]{2,1,0:T(8,128)(2,1)} %get-tuple-element.9) | copy-start | bytes 3145732
  108.2 1.7 %copy-start.1 = (bf16[32,128,128]{2,1,0:T(8,128)(2,1)S(1)}, bf16[32,128,128]{2,1,0:T(8,128)(2,1)}, u32[]{:S(2)}) copy-start(bf16[32,128,128]{2,1,0:T(8,128)(2,1)} %get-tuple-element.10) | copy-start | bytes 3145732
  109.9 1.7 %copy-start = (bf16[32,128,128]{2,1,0:T(8,128)(2,1)S(1)}, bf16[32,128,128]{2,1,0:T(8,128)(2,1)}, u32[]{:S(2)}) copy-start(bf16[32,128,128]{2,1,0:T(8,128)(2,1)} %get-tuple-element.11) | copy-start | bytes 3145732

commit v2 on v0

v2 whole, which is shorter than its diff:
```python
import jax
import jax.numpy as jnp
from jax import lax
from jax.experimental import pallas as pl
from jax.experimental.pallas import tpu as pltpu
from jax.sharding import PartitionSpec as P

MESH = pl.DeviceIdType.MESH
NZ, NY, NCORE, NX = 8, 4, 2, 4
ROW = NCORE * NX
PLANE = NY * ROW
GROUPS = 4
NEAR_ROW = (0, 4, 1, 5, 3, 7, 2, 6)
NEAR_Y = (0, 1, 3, 2)
LATER = (("states", 0), ("inside", 2), ("fold", 3), ("inc", 5), ("out", 7), ("grads", 9), ("fold_back", 10),
         ("inc_back", 12), ("fin", 14))
F32 = jnp.float32
BF16 = jnp.bfloat16


def dot(a, b, ca, cb):
    return lax.dot_general(a, b, (((ca,), (cb,)), ((), ())), preferred_element_type=F32)


def kernel(
    rate_ref, gain_ref, q_hbm, k_hbm, v_hbm, g_hbm,
    normed_hbm, dq_hbm, dk_hbm, dv_hbm,
    tok, q_ref, k_ref, v_ref, g_ref, normed_ref, dq_ref, dk_ref, dv_ref,
    masks, heads_decay, tails_decay, att, intra, go, dk_part, dv_part,
    ls, lr, ins, inr, gs, gr, lts, ltr, cs, cr, csb, crb,
    s_row, r_row, s_z, r_z, in_sem, out_sem,
):
    ctx = lax.axis_index("ctx")
    x = lax.axis_index("head")
    z, y, core = ctx // (NY * NCORE), (ctx // NCORE) % NY, ctx % NCORE
    row = core * NX + x
    me = y * ROW + row
    heads, size = q_ref.shape[0], q_ref.shape[1]
    per = heads // GROUPS
    cut = PLANE // per
    depth = size // cut

    loads = [pltpu.make_async_copy(a, tok.at[n], in_sem.at[n]) for n, a in enumerate((k_hbm, v_hbm, q_hbm, g_hbm))]
    for load in loads:
        load.start()

    ys = [(y + d) % NY for d in range(NY)]
    rows = [(row + d) % ROW for d in range(ROW)]
    cores = [a // NX for a in rows]
    xs = [a % NX for a in rows]

    def plane_device(dy, dr):
        return ((z * NY + ys[dy]) * NCORE + cores[dr], xs[dr])

    def z_device(z2):
        return ((z2 * NY + y) * NCORE + core, x)

    cr[...] = jnp.zeros_like(cr)
    crb[...] = jnp.zeros_like(crb)

    others = [(dy, dr) for dy in reversed(NEAR_Y) for dr in reversed(NEAR_ROW) if dy or dr]
    barrier = pltpu.get_barrier_semaphore()
    for dy, dr in others:
        pl.semaphore_signal(barrier, inc=1, device_id=plane_device(dy, dr), device_id_type=MESH)
    for d in range(1, NZ):
        pl.semaphore_signal(barrier, inc=1, device_id=z_device((z + d) % NZ), device_id_type=MESH)

    half = heads // 2
    for n, ref in enumerate((k_ref, v_ref, q_ref, g_ref)):
        loads[n].wait()
        for hh in range(2):
            @pl.loop(0, size // 16)
            def _(t):
                ref[pl.ds(hh * half, half), pl.ds(t * 16, 16), :] = jnp.transpose(
                    tok[n, pl.ds(t * 16, 16), pl.ds(hh * half, half), :], (1, 0, 2))

    pl.semaphore_wait(barrier, PLANE + NZ - 2)

    step_i = lax.broadcasted_iota(jnp.int32, (size, size), 0).astype(F32)
    step_j = lax.broadcasted_iota(jnp.int32, (size, size), 1).astype(F32)

    def span_decay(rate, stretches):
        return jnp.exp(jnp.full((1, size), -rate * (1.0 * size * stretches), F32))

    def plane_copy(src, dst, phase, g, dy, dr):
        return pltpu.make_async_remote_copy(
            src_ref=src.at[g, ys[dy] * ROW + rows[dr]], dst_ref=dst.at[g, me],
            send_sem=s_row.at[phase, g], recv_sem=r_row.at[phase, g],
            device_id=plane_device(dy, dr), device_id_type=MESH)

    def plane_all(src, dst, phase, g):
        return pltpu.make_async_remote_copy(
            src_ref=src.at[g, pl.ds(0, PLANE - 1)], dst_ref=dst.at[g, pl.ds(0, PLANE - 1)],
            send_sem=s_row.at[phase, g], recv_sem=r_row.at[phase, g],
            device_id=plane_device(0, 1), device_id_type=MESH)

    def send(src, dst, phase, g):
        for dy, dr in others:
            plane_copy(src, dst, phase, g, dy, dr).start()
        dst[g, me] = src[g, me]

    def z_copy(src, dst, way, g, d, sending):
        towards = d if way == 0 else -d
        z2 = z + towards if sending else z - towards
        slot = z if sending else z2
        there = jnp.logical_and(z2 >= 0, z2 < NZ)
        return there, pltpu.make_async_remote_copy(
            src_ref=src.at[g], dst_ref=dst.at[g, slot],
            send_sem=s_z.at[way, g, d], recv_sem=r_z.at[way, g, d],
            device_id=z_device(z2), device_id_type=MESH)

    def fold(own, got, c_out, c_in, phase, way, g):
        plane_all(own, got, phase, g).wait_recv()
        weight = span_decay(rate_ref[g * per + me // cut], 1)
        order = range(PLANE) if way == 0 else range(PLANE - 1, -1, -1)
        acc = None
        for c in order:
            piece = got[g, c].astype(F32)
            acc = piece if acc is None else acc * weight + piece
        c_out[g] = acc.astype(BF16)
        for d in range(1, NZ):
            there, copy = z_copy(c_out, c_in, way, g, d, True)

            @pl.when(there)
            def _():
                copy.start()

    def inc(own, got, c_out, c_in, out, back, phase, way, g):
        for d in range(1, NZ):
            there, copy = z_copy(c_out, c_in, way, g, d, False)

            @pl.when(there)
            def _():
                copy.wait_recv()

        rate = rate_ref[g * per + me // cut]
        weight = span_decay(rate, 1)
        plane = span_decay(rate, PLANE)
        acc = jnp.zeros((depth, size), F32)
        for d in range(NZ - 1, 0, -1):
            z2 = (z + NZ - d) % NZ if way == 0 else (z + d) % NZ
            acc = acc * plane + c_in[g, z2].astype(F32)
        order = range(PLANE) if way == 0 else range(PLANE - 1, -1, -1)
        for c in order:
            out[g, c] = acc.astype(BF16)
            acc = acc * weight + got[g, c].astype(F32)
        send(out, back, phase, g)

    def each_head(g, body):
        @pl.loop(0, per // 4)
        def _(i):
            for j in range(4):
                body(g * per + i * 4 + j, i * 4 + j)

    def put(dst, g, n, state):
        dst[g, pl.ds(n * cut, cut)] = state.astype(BF16).reshape(cut, depth, size)

    def take(src, g, n):
        return src[g, pl.ds(n * cut, cut)].reshape(size, size)

    def results_copy(n, hbm, hh):
        part = pl.ds(hh * half, half)
        return pltpu.make_async_copy(tok.at[n, :, part], hbm.at[:, part], out_sem.at[n, hh])

    def results_out(n, ref, hbm, g):
        @pl.when((g + 1) * per % half == 0)
        def _():
            hh = g * per // half

            @pl.loop(0, size // 16)
            def _(t):
                tok[n, pl.ds(t * 16, 16), pl.ds(hh * half, half), :] = jnp.transpose(
                    ref[pl.ds(hh * half, half), pl.ds(t * 16, 16), :], (1, 0, 2))
            results_copy(n, hbm, hh).start()

    def states(g):
        def body(h, n):
            tail = jnp.exp(-rate_ref[h] * (size - 1.0 - step_i))
            tails_decay[h] = tail
            key_decayed = (k_ref[h].astype(F32) * tail).astype(BF16)
            put(ls, g, n, dot(key_decayed, v_ref[h], 0, 0))
        each_head(g, body)
        send(ls, lr, 0, g)

    def inside(g):
        def body(h, n):
            offset = step_i - step_j
            mask = jnp.where(offset >= 0, jnp.exp(-rate_ref[h] * jnp.maximum(offset, 0.0)), 0.0)
            masks[h] = mask
            weights = (dot(q_ref[h], k_ref[h], 1, 1) * mask).astype(BF16)
            att[h] = weights
            intra[h] = dot(weights, v_ref[h], 1, 0)
        each_head(g, body)

    def out(g):
        plane_all(ins, inr, 1, g).wait_recv()

        def body(h, n):
            decay = jnp.exp(-rate_ref[h] * (step_i + 1.0))
            heads_decay[h] = decay
            queries = q_ref[h]
            outputs = intra[h] + decay * dot(queries, take(inr, g, n), 1, 0)
            inv_rms = lax.rsqrt(jnp.mean(outputs * outputs, axis=-1, keepdims=True) + 1e-06)
            unit = outputs * inv_rms
            gain = gain_ref[h]
            normed_ref[h] = (unit * gain).astype(BF16)
            scaled = gain * g_ref[h].astype(F32)
            grad_out = (
                inv_rms * (scaled - unit * jnp.mean(scaled * unit, axis=-1, keepdims=True))
            ).astype(BF16)
            go[h] = grad_out
            query_decayed = (queries.astype(F32) * decay).astype(BF16)
            put(gs, g, n, dot(query_decayed, grad_out, 0, 0))
        each_head(g, body)
        send(gs, gr, 2, g)
        results_out(0, normed_ref, normed_hbm, g)

    def grads(g):
        def body(h, n):
            grad_out = go[h]
            score_grad = (dot(grad_out, v_ref[h], 1, 1) * masks[h]).astype(BF16)
            dq = dot(score_grad, k_ref[h], 1, 0)
            dq = dq + heads_decay[h] * dot(grad_out, take(inr, g, n), 1, 1)
            dq_ref[h] = dq.astype(BF16)
            dk_part[h] = dot(score_grad, q_ref[h], 0, 0)
            dv_part[h] = dot(att[h], grad_out, 0, 0)
        each_head(g, body)
        results_out(1, dq_ref, dq_hbm, g)

    def fin(g):
        plane_all(lts, ltr, 3, g).wait_recv()

        def body(h, n):
            decay = tails_decay[h]
            later = take(ltr, g, n)
            dk_ref[h] = (dk_part[h] + decay * dot(v_ref[h], later, 1, 1)).astype(BF16)
            dv_ref[h] = (dv_part[h] + decay * dot(k_ref[h], later, 1, 0)).astype(BF16)
        each_head(g, body)
        results_out(2, dk_ref, dk_hbm, g)
        results_out(3, dv_ref, dv_hbm, g)

    stages = {
        "states": states,
        "inside": inside,
        "fold": lambda g: fold(ls, lr, cs, cr, 0, 0, g),
        "inc": lambda g: inc(ls, lr, cs, cr, ins, inr, 1, 0, g),
        "out": out,
        "grads": grads,
        "fold_back": lambda g: fold(gs, gr, csb, crb, 2, 1, g),
        "inc_back": lambda g: inc(gs, gr, csb, crb, lts, ltr, 3, 1, g),
        "fin": fin,
    }

    @pl.loop(0, GROUPS + max(late for _, late in LATER))
    def _(s):
        for name, late in LATER:
            @pl.when(jnp.logical_and(s >= late, s < late + GROUPS))
            def _():
                stages[name](s - late)

    @pl.loop(0, GROUPS)
    def _(g):
        for phase, (src, dst) in enumerate(((ls, lr), (ins, inr), (gs, gr), (lts, ltr))):
            plane_all(src, dst, phase, g).wait_send()
        for way, (src, dst) in enumerate(((cs, cr), (csb, crb))):
            for d in range(1, NZ):
                there, copy = z_copy(src, dst, way, g, d, True)

                @pl.when(there)
                def _():
                    copy.wait_send()

    for n, hbm in enumerate((normed_hbm, dq_hbm, dk_hbm, dv_hbm)):
        for hh in range(2):
            results_copy(n, hbm, hh).wait()


def hand_on(*refs):
    results, outs, (held, in_sem, out_sem) = refs[:4], refs[4:8], refs[8:]
    chunks = in_sem.shape[1]
    rows = held.shape[1] // chunks
    parts = [(n, c, pl.ds(c * rows, rows)) for c in range(chunks) for n in range(4)]
    loads = [pltpu.make_async_copy(results[n].at[part], held.at[n, part], in_sem.at[n, c]) for n, c, part in parts]
    stores = [pltpu.make_async_copy(held.at[n, part], outs[n].at[part], out_sem.at[n, c]) for n, c, part in parts]
    for load in loads:
        load.start()
    for load, store in zip(loads, stores):
        load.wait()
        store.start()
    for store in stores:
        store.wait()


def local(queries, key_vectors, value_vectors, output_grad, decay_rate, norm_gain):
    length, heads, size = queries.shape
    tile = (size, size)
    every = lambda dtype: pltpu.VMEM((heads,) + tile, dtype)
    depth = size * heads // GROUPS // PLANE
    pieces = pltpu.VMEM((GROUPS, PLANE, depth, size), BF16)
    columns = [pltpu.VMEM((GROUPS, depth, size), BF16), pltpu.VMEM((GROUPS, NZ, depth, size), BF16)]
    by_token = jax.ShapeDtypeStruct((length, heads, size), BF16)
    results = pl.pallas_call(
        kernel,
        out_shape=[by_token] * 4,
        in_specs=[pl.BlockSpec(memory_space=pltpu.SMEM), pl.BlockSpec(memory_space=pltpu.VMEM)]
        + [pl.BlockSpec(memory_space=pl.ANY)] * 4,
        out_specs=[pl.BlockSpec(memory_space=pl.ANY)] * 4,
        scratch_shapes=[pltpu.VMEM((4, length, heads, size), BF16)]
        + [every(BF16)] * 8
        + [every(F32)] * 3
        + [every(BF16), every(F32), every(BF16), every(F32), every(F32)]
        + [pieces] * 8
        + columns + columns
        + [
            pltpu.SemaphoreType.DMA((4, GROUPS)),
            pltpu.SemaphoreType.DMA((4, GROUPS)),
            pltpu.SemaphoreType.DMA((2, GROUPS, NZ)),
            pltpu.SemaphoreType.DMA((2, GROUPS, NZ)),
            pltpu.SemaphoreType.DMA((4,)),
            pltpu.SemaphoreType.DMA((4, 2)),
        ],
        compiler_params=pltpu.CompilerParams(
            collective_id=0, has_side_effects=True, vmem_limit_bytes=60 * 1024 * 1024
        ),
    )(decay_rate, norm_gain.reshape(heads, 1, size), queries, key_vectors, value_vectors, output_grad)
    return tuple(pl.pallas_call(
        hand_on,
        out_shape=[by_token] * 4,
        in_specs=[pl.BlockSpec(memory_space=pl.ANY)] * 4,
        out_specs=[pl.BlockSpec(memory_space=pl.ANY)] * 4,
        scratch_shapes=[
            pltpu.VMEM((4, length, heads, size), BF16),
            pltpu.SemaphoreType.DMA((4, 4)),
            pltpu.SemaphoreType.DMA((4, 4)),
        ],
        compiler_params=pltpu.CompilerParams(vmem_limit_bytes=60 * 1024 * 1024),
    )(*results))


def solution(mesh):
    spec = P(("ctx", "head"), None, None)
    return jax.shard_map(
        local, mesh=mesh, in_specs=(spec,) * 4 + (P(), P()), out_specs=(spec,) * 4, check_vma=False
    )
```

time: 295 us -> 73.6 us (0.25)
  other arithmetic: 106 us -> 0 us
  waiting for transfers between devices: 79 us -> 0 us
  Pallas kernels: 0 us -> 72.8 us
  starting transfers between devices: 46.3 us -> 0 us
  matrix products: 35.3 us -> 0 us
  local copies, waits for them, and re-layouts: 24.2 us -> 0 us
    all_to_all x8 -> x0, waiting for transfers between devices: 79 us -> none  [the longest x2 25.4 us: carry_states(): lax.all_to_all(flat_rows, 'ctx', split_axis=1, concat_axis=0, tiled=True)]
    pallas_call x0 -> x2, Pallas kernels: none -> 72.8 us  [the longest x1 68.9 us: local(): pl.pallas_call(kernel, out_shape=[by_token] * 4, in_specs=[pl.BlockSpec(m...]
    add x128 -> x0, other arithmetic: 53.3 us -> none  [carry_step(): return (row_decay * state + piece.astype(jnp.float32), state)]
    all_to_all x8 -> x0, starting transfers between devices: 46.3 us -> none  [the longest x2 20.5 us: carry_states(): lax.all_to_all(flat_rows, 'ctx', split_axis=1, concat_axis=0, tiled=True)]
    dynamic_update_slice x128 -> x0, other arithmetic: 39 us -> none  [local_chain(): lax.scan(carry_step, empty_rows, spread_rows, reverse=not forward)]
    dot_general x16 -> x0, matrix products: 35.3 us -> none  [the longest x1 3.69 us: local(): jnp.einsum('khij,kihd->kjhd', score_gradient, query_stretches, preferred_...]
    unnamed x48 -> x0, local copies, waits for them, and re-layouts: 19.1 us -> none
    unnamed x4 -> x0, other arithmetic: 5.14 us -> none
  transfers between devices with their start and end apart: 8 -> 0, of which waited for: 8 -> 0; matrix products, arithmetic and copies ran while one was open for 10% -> 0% of each run, Pallas kernels for 0% -> 0%
where the time goes in v2:
time: 73.6 us; the launch traced here: 73.4 us
  Pallas kernels  72.8 us (99%)
    pallas_call x1, Pallas kernels, local(): pl.pallas_call(kernel, out_shape=[by_token] * 4, in_specs=[pl.BlockSpec(m...  68.9 us
    pallas_call x1, Pallas kernels, local(): pl.pallas_call(hand_on, out_shape=[by_token] * 4, in_specs=[pl.BlockSpec(...  3.85 us

profile of v2, /device:TPU:1, one launch (start us, length us, event | category | flops | bytes accessed | tf_op | source)
XLA Modules:
  0.0 73.4 jit_solution(13807505121051353571)
XLA Ops:
  0.6 68.9 %shard_map.93 = (bf16[128,32,128]{2,1,0:T(8,128)(2,1)}, bf16[128,32,128]{2,1,0:T(8,128)(2,1)}, bf16[128,32,128]{2,1,0:T(8,128)(2,1)}, bf16[128,32,128]{2,1,0:T(8,128)(2,1)}) custom-call(f32[32]{0:T(128)} %rate_ref.1, f32[32,1,128]{2,1,0:T(1,128)} %bitcast.1, bf16[128,32,128]{2,1,0:T(8,128)(2,1)} %q_hbm.1, bf16[128,32,128]{2,1,0:T(8,128)(2,1)} %k_hbm.1, ...), custom_call_target="tpu_custom_call" | custom-call | tf_op jit(solution)/shard_map/pallas_call | solution.py:302
  69.6 3.9 %shard_map.94 = (bf16[128,32,128]{2,1,0:T(8,128)(2,1)}, bf16[128,32,128]{2,1,0:T(8,128)(2,1)}, bf16[128,32,128]{2,1,0:T(8,128)(2,1)}, bf16[128,32,128]{2,1,0:T(8,128)(2,1)}) custom-call(bf16[128,32,128]{2,1,0:T(8,128)(2,1)} %get-tuple-element.8.refs_0_, bf16[128,32,128]{2,1,0:T(8,128)(2,1)} %get-tuple-element.9.refs_1_, ...), custom_call_target="tpu_custom_call" | custom-call | tf_op jit(solution)/shard_map/pallas_call | solution.py:326
